TPU v7x, 128 devices: a whole 4x4x4 slice. The times are simulated.
128 devices in a mesh: pr: 16 (over z, x), pc: 8 (over y, core).
Axes of the slice: x: 4, y: 4, z: 4, core: 2. Of those that a mesh axis runs over, the one named last changes fastest.
Arguments:
- trailing: float32 [20480, 20480], P('pr', 'pc'), may hold values from -25 to 25, as said below
- v_panels: float32 [6, 32, 20480], P(None, None, ('pr', 'pc')), may hold values from -0.078125 to 0.078125
- t_panels: float32 [6, 32, 32], replicated, may hold values from -0.2 to 0.5, as said below
Outputs:
- updated: float32 [20480, 20480], P('pr', 'pc')
- w_panels: float32 [6, 32, 20480], P(None, None, ('pr', 'pc'))
Inputs may be any that keep to these rules, and one draw needn't show every extreme that they name: trailing is exactly symmetric. `t_panels`: each panel's factor is upper triangular with diagonal entries of 0.25 to 0.5.
All inputs are finite; a program needn't handle non-finite values.
Results may differ from a plain program's by a relative error of at most 0.00013.
Values sent between devices are 32-bit elements; how exact they have to be, the bound alone decides.
A program may use at most 128 MiB of HBM per device.

v0:
```python
import jax
import jax.numpy as jnp
from jax import lax
from jax.sharding import PartitionSpec as P

HIGHEST = lax.Precision.HIGHEST


def contract(left_side, right_side, left_dim, right_dim, precision=HIGHEST):
    return lax.dot_general(
        left_side,
        right_side,
        (((left_dim,), (right_dim,)), ((), ())),
        precision=precision,
        preferred_element_type=jnp.float32,
    )


def small_coefficients(gram_y, gram_v, t_panels):
    panels, width, _ = t_panels.shape
    size = panels * width
    eye = jnp.eye(size, dtype=jnp.float32)
    zero = jnp.zeros((size, size), jnp.float32)
    of_y = jnp.concatenate([gram_y, zero, eye], axis=1)
    of_v = jnp.concatenate([gram_v, eye, zero], axis=1)
    of_w = []
    for panel in range(panels):
        here = slice(panel * width, (panel + 1) * width)
        of_x = of_y[here]
        if panel:
            done = jnp.concatenate(of_w, axis=0)
            before = slice(0, panel * width)
            left = jnp.concatenate([done[:, here], gram_v[before, here]], axis=0)
            right = jnp.concatenate([of_v[before], done], axis=0)
            of_x = of_x - contract(left, right, 0, 0)
        factor = t_panels[panel]
        scaled = contract(factor, of_x, 0, 0)
        middle = contract(scaled[:, here], factor, 1, 0)
        of_w.append(scaled - 0.5 * contract(middle, of_v[here], 1, 0))
    return jnp.concatenate(of_w, axis=0)


def per_device(trailing, v_panels, t_panels):
    rows, cols = (lax.axis_size("pr"), lax.axis_size("pc"))
    ratio = rows // cols
    panels, width, share = v_panels.shape
    size = panels * width
    v_own = v_panels.reshape(size, share)
    moves = []
    for i in range(rows):
        for j in range(cols):
            moves.append((i * cols + j, (i % ratio * cols + j) * cols + i // ratio))

    def columns(own):
        return lax.all_gather(lax.ppermute(own, ("pr", "pc"), moves), "pr", axis=1, tiled=True)

    v_row = lax.all_gather(v_own, "pc", axis=1, tiled=True)
    v_col = columns(v_own)
    partial_y = contract(v_col, trailing, 1, 1, lax.Precision.HIGH)
    y_own = lax.psum_scatter(partial_y, "pc", scatter_dimension=1, tiled=True)
    y_row = lax.all_gather(y_own, "pc", axis=1, tiled=True)
    y_col = columns(y_own)
    grams = contract(v_own, jnp.concatenate([y_own, v_own], axis=0), 1, 1)
    grams = lax.psum(grams, ("pr", "pc"))
    coefs = small_coefficients(grams[:, :size], grams[:, size:], t_panels)
    of_v, of_y = (coefs[:, size : 2 * size], coefs[:, 2 * size :])
    w_own = contract(of_v, v_own, 1, 0) + contract(of_y, y_own, 1, 0)
    left_v = contract(of_v + of_v.T, v_row, 1, 0) + contract(of_y, y_row, 1, 0)
    left_y = contract(of_y, v_row, 0, 0)
    left = jnp.concatenate([left_v, left_y], axis=0)
    right = jnp.concatenate([v_col, y_col], axis=0)
    matrix = trailing - contract(left, right, 0, 0, lax.Precision.HIGH)
    return (matrix, w_own.reshape(panels, width, share))


def solution(mesh):
    return jax.shard_map(
        per_device,
        mesh=mesh,
        in_specs=(P("pr", "pc"), P(None, None, ("pr", "pc")), P()),
        out_specs=(P("pr", "pc"), P(None, None, ("pr", "pc"))),
        check_vma=False,
    )
```

profile of v0, /device:TPU:1, one launch (start us, length us, event | category | flops | bytes accessed | tf_op | source)
XLA Modules:
  0.0 353.8 jit_solution(15385846826090534265)
XLA Ops:
  8.2 4.5 %collective-permute-start = (f32[192,160]{0,1:T(8,128)S(1)}, f32[192,160]{0,1:T(8,128)S(1)}, u32[]{:S(2)}, u32[]{:S(2)}) collective-permute-start(f32[192,160]{0,1:T(8,128)S(1)} %copy.12), channel_id=1, source_target_pairs={{0,0},{1,8},{2,16},{3,24},{4,32},{5,40},{6,48},{7,56},{8,64},{9,72... | collective-permute-start | bytes 368648 | tf_op jit(solution)/shard_map/ppermute | solution.py:55
  12.8 4.5 %collective-permute-done = f32[192,160]{0,1:T(8,128)S(1)} collective-permute-done((f32[192,160]{0,1:T(8,128)S(1)}, f32[192,160]{0,1:T(8,128)S(1)}, u32[]{:S(2)}, u32[]{:S(2)}) %collective-permute-start) | collective-permute-done | bytes 122912 | tf_op jit(solution)/shard_map/ppermute | solution.py:55
  18.0 53.5 %all-gather.3.cloned.1.call-done = f32[192,2560]{0,1:T(8,128)} async-done(((f32[192,160]{0,1:T(8,128)}), f32[192,2560]{0,1:T(8,128)}) %all-gather.3.cloned.1.call-update) | async-done | bytes 1966096 | tf_op jit(solution)/shard_map/all_gather | solution.py:55
  71.5 9.9 %fusion.106 = f32[192,1280]{0,1:T(8,128)} fusion(f32[192,2560]{0,1:T(8,128)} %all-gather.3.cloned.1.call-done, f32[1280,2560]{1,0:T(8,128)} %param.3), kind=kOutput, calls=%fused_computation.158 | convolution fusion | flops 3774873600 | bytes 16056320 | tf_op jit(solution)/shard_map/dot_general | solution.py:10
  82.2 15.8 %all_gather.13 = f32[192,1280]{0,1:T(8,128)S(1)} all-gather(f32[192,160]{0,1:T(8,128)S(1)} %copy.12), channel_id=1, replica_groups=mesh['pr'=16,'pc'=8] {'pc'}, dimensions={1}, use_global_device_ids=true | all-gather | bytes 1105920 | tf_op jit(solution)/shard_map/all_gather | solution.py:57
  98.0 13.6 %reduce-scatter.2.cloned.1.call-done = f32[192,160]{0,1:T(8,128)} async-done(((f32[192,1280]{0,1:T(8,128)}), f32[192,160]{0,1:T(8,128)}) %reduce-scatter.2.cloned.1.call-update) | async-done | bytes 122896 | tf_op jit(solution)/shard_map/reduce_scatter | solution.py:60
  111.6 2.2 convolution_bitcast_fusion
  113.9 6.3 %collective-permute-start.1 = (f32[192,160]{0,1:T(8,128)}, f32[192,160]{0,1:T(8,128)S(1)}, u32[]{:S(2)}, u32[]{:S(2)}) collective-permute-start(f32[192,160]{0,1:T(8,128)} %reduce-scatter.2.cloned.1.call-done), channel_id=1, source_target_pairs={{0,0},{1,8},{2,16},{3,24},{4,32},{5,40},{6,48},{7,56},{8,64},{9,72... | collective-permute-start | bytes 368648 | tf_op jit(solution)/shard_map/ppermute | solution.py:55
  120.2 20.7 %all_gather.14 = f32[192,1280]{0,1:T(8,128)S(1)} all-gather(f32[192,160]{0,1:T(8,128)} %reduce-scatter.2.cloned.1.call-done), channel_id=1, replica_groups=mesh['pr'=16,'pc'=8] {'pc'}, dimensions={1}, use_global_device_ids=true | all-gather | bytes 1105920 | tf_op jit(solution)/shard_map/all_gather | solution.py:61
  141.6 118.4 %all-reduce.2.cloned.1.call-done = f32[192,384]{1,0:T(8,128)} async-done(((f32[192,384]{1,0:T(8,128)}), f32[192,384]{1,0:T(8,128)}) %all-reduce.2.cloned.1.call-update) | async-done | bytes 294928 | tf_op jit(solution)/shard_map/psum | solution.py:64
  260.0 1.1 fusion.105
  261.2 2.0 pad_maximum_fusion.1
  269.1 1.2 convolution_bitcast_fusion.6
  272.9 1.2 convolution_subtract_fusion.3
  277.9 1.3 convolution_subtract_fusion.5
  282.8 1.5 copy.16
  284.2 1.5 convolution_subtract_fusion.4
  287.4 1.5 fusion.60
  288.9 1.5 slice.195
  290.5 1.5 copy.19
  292.0 1.6 slice.201
  293.6 1.6 copy.21
  295.2 1.9 constant_dynamic-update-slice_fusion.5
  298.6 1.6 convolution_subtract_fusion.2
  304.6 1.8 convolution_subtract_fusion.1
  309.2 1.1 slice.205
  310.3 1.3 fusion.30
  311.5 1.6 convolution_add_fusion.1
  314.0 3.9 %fusion.32 = f32[192,1280]{1,0:T(8,128)} fusion(f32[192,1280]{0,1:T(8,128)S(1)} %all_gather.13, f32[192,576]{1,0:T(8,128)} %fusion.7), kind=kOutput, calls=%fused_computation.59 | convolution fusion | flops 566231040 | bytes 2162688 | tf_op jit(solution)/shard_map/dot_general | solution.py:10
  317.9 2.4 fusion.28
  320.4 3.4 convolution_add_fusion
  323.8 23.5 %convolution_subtract_fusion = f32[1280,2560]{1,0:T(8,128)} fusion(f32[1280,2560]{1,0:T(8,128)} %param.3, f32[192,2560]{0,1:T(8,128)} %all-gather.5.cloned.1.call-done, f32[192,2560]{0,1:T(8,128)} %all-gather.3.cloned.1.call-done, f32[192,1280]{1,0:T(8,128)S(1)} %copy-done, f32[192,1280]{1,0:T(8,128)} %convolution_add_fusion), kind=kOutput, calls=%fused_computation | convolution fusion | flops 7554498560 | bytes 32112640 | tf_op jit(solution)/shard_map/dot_general | solution.py:10
  (62 shorter events, 30.5 us)
Async XLA Ops:
  7.2 64.3 %all-gather.3.cloned.1.call-start = ((), (), s32[]{:S(2)}) async-start(), calls=%async_computation.1 | async-start | bytes 2785280 | tf_op jit(solution)/shard_map/all_gather | solution.py:55
  8.2 9.0 %collective-permute-start = (f32[192,160]{0,1:T(8,128)S(1)}, f32[192,160]{0,1:T(8,128)S(1)}, u32[]{:S(2)}, u32[]{:S(2)}) collective-permute-start(f32[192,160]{0,1:T(8,128)S(1)} %copy.12), channel_id=1, source_target_pairs={{0,0},{1,8},{2,16},{3,24},{4,32},{5,40},{6,48},{7,56},{8,64},{9,72... | collective-permute-start | bytes 368648 | tf_op jit(solution)/shard_map/ppermute | solution.py:55
  17.3 0.7 copy-start.5
  18.0 93.6 %reduce-scatter.2.cloned.1.call-start = ((), (), s32[]{:S(2)}) async-start(), calls=%async_computation.2 | async-start | bytes 1474560 | tf_op jit(solution)/shard_map/reduce_scatter | solution.py:60
  81.4 30.2 %copy-start.1 = (f32[6,32,160]{2,1,0:T(8,128)S(1)}, f32[6,32,160]{2,1,0:T(8,128)}, u32[]{:S(2)}) copy-start(f32[6,32,160]{2,1,0:T(8,128)} %param.4) | copy-start | bytes 368644
  81.5 178.6 %all-reduce.2.cloned.1.call-start = ((), (), s32[]{:S(2)}) async-start(), calls=%async_computation.3 | async-start | bytes 589824 | tf_op jit(solution)/shard_map/psum | solution.py:64
  113.8 210.0 %all-gather.5.cloned.1.call-start = ((), (), s32[]{:S(2)}) async-start(), calls=%async_computation.4 | async-start | bytes 2785280 | tf_op jit(solution)/shard_map/all_gather | solution.py:55
  113.9 27.0 %collective-permute-start.1 = (f32[192,160]{0,1:T(8,128)}, f32[192,160]{0,1:T(8,128)S(1)}, u32[]{:S(2)}, u32[]{:S(2)}) collective-permute-start(f32[192,160]{0,1:T(8,128)} %reduce-scatter.2.cloned.1.call-done), channel_id=1, source_target_pairs={{0,0},{1,8},{2,16},{3,24},{4,32},{5,40},{6,48},{7,56},{8,64},{9,72... | collective-permute-start | bytes 368648 | tf_op jit(solution)/shard_map/ppermute | solution.py:55
  140.9 0.7 copy-start.4
  277.0 0.8 copy-start.6
  286.8 0.6 copy-start.3
  297.7 12.6 %copy-start.2 = (f32[192,160]{0,1:T(8,128)S(1)}, f32[192,160]{0,1:T(8,128)}, u32[]{:S(2)}) copy-start(f32[192,160]{0,1:T(8,128)} %reduce-scatter.2.cloned.1.call-done) | copy-start | bytes 368644
  320.3 3.4 copy-start
Sparse Core Ops, SparseCore 0:
  18.1 53.3 all-gather.2
  81.6 29.9 reduce-scatter.1
  116.9 143.0 all-reduce.1
  262.0 44.4 all-gather.4
where the time goes:
time: 355 us; the launch traced here: 354 us
  waiting for transfers between devices  190 us (54%)
  matrix products  74.1 us (21%)
  blocking collectives  36.6 us (10%)
  local copies, waits for them, and re-layouts  24.1 us (7%)
  between operations  14 us (4%)
  starting transfers between devices  11 us (3%)
  other arithmetic  4.12 us (1%)
    psum x1, waiting for transfers between devices, per_device(): grams = lax.psum(grams, ('pr', 'pc'))  118 us
    dot_general x31, matrix products, contract(): lax.dot_general(left_side, right_side, (((left_dim,), (right_dim,)), ((),...  74.1 us
    all_gather x2, waiting for transfers between devices, columns(): lax.all_gather(lax.ppermute(own, ('pr', 'pc'), moves), 'pr', axis=1, tile...  53.5 us
    all_gather x1, blocking collectives, per_device(): y_row = lax.all_gather(y_own, 'pc', axis=1, tiled=True)  20.7 us
    all_gather x1, blocking collectives, per_device(): v_row = lax.all_gather(v_own, 'pc', axis=1, tiled=True)  15.8 us
    slice x15, local copies, waits for them, and re-layouts, small_coefficients(): left = jnp.concatenate([done[:, here], gram_v[before, here]], axis=0)  14.3 us
    reduce_scatter x1, waiting for transfers between devices, per_device(): y_own = lax.psum_scatter(partial_y, 'pc', scatter_dimension=1, tiled=True)  13.6 us
    ppermute x2, starting transfers between devices, columns(): lax.ppermute(own, ('pr', 'pc'), moves)  10.8 us
  transfers between devices with their start and end apart: 6, of which 4 were waited for; matrix products, arithmetic and copies ran while one was open for 18% of the time, Pallas kernels for 0%

commit v1 on v0

--- a/solution.py
+++ b/solution.py
@@ -54,7 +54,14 @@
     def columns(own):
         return lax.all_gather(lax.ppermute(own, ("pr", "pc"), moves), "pr", axis=1, tiled=True)
 
-    v_row = lax.all_gather(v_own, "pc", axis=1, tiled=True)
+    peers = lax.axis_size("pc")
+    route = [(i_2, (i_2 + 1) % peers) for i_2 in range(peers)]
+    pieces = [v_own]
+    for far in range(1, peers):
+        pieces = [lax.ppermute(pieces[0], "pc", route), *pieces]
+    whole = jnp.concatenate(pieces, axis=1)
+    shift = (lax.axis_index("pc") + 1) * pieces[-1].shape[1]
+    v_row = jnp.roll(whole, shift, axis=1)
     v_col = columns(v_own)
     partial_y = contract(v_col, trailing, 1, 1, lax.Precision.HIGH)
     y_own = lax.psum_scatter(partial_y, "pc", scatter_dimension=1, tiled=True)

time: 355 us -> 351 us (0.989)
  blocking collectives: 36.6 us -> 20.2 us
  starting transfers between devices: 11 us -> 25.6 us
  waiting for transfers between devices: 190 us -> 202 us
  local copies, waits for them, and re-layouts: 24.1 us -> 16.1 us
  matrix products: 74.1 us -> 69 us
    ppermute x0 -> x7, waiting for transfers between devices: none -> 29.8 us  [per_device(): pieces = [lax.ppermute(pieces[0], 'pc', route), *pieces]]
    all_gather x1 -> x0, blocking collectives: 15.8 us -> none  [per_device(): v_row = lax.all_gather(v_own, 'pc', axis=1, tiled=True)]
    reduce_scatter x1, waiting for transfers between devices: 13.6 us -> 0.02 us  [per_device(): y_own = lax.psum_scatter(partial_y, 'pc', scatter_dimension=1, tiled=True)]
    ppermute x0 -> x7, starting transfers between devices: none -> 13 us  [per_device(): pieces = [lax.ppermute(pieces[0], 'pc', route), *pieces]]
    slice x15, local copies, waits for them, and re-layouts: 14.3 us -> 4.57 us  [small_coefficients(): left = jnp.concatenate([done[:, here], gram_v[before, here]], axis=0)]
    dot_general x31, matrix products: 74.1 us -> 69 us  [contract(): lax.dot_general(left_side, right_side, (((left_dim,), (right_dim,)), ((),...]
    psum x1, waiting for transfers between devices: 118 us -> 114 us  [per_device(): grams = lax.psum(grams, ('pr', 'pc'))]
  transfers between devices with their start and end apart: 6 -> 13, of which waited for: 4 -> 10; matrix products, arithmetic and copies ran while one was open for 18% -> 14% of each run, Pallas kernels for 0% -> 0%
where the time goes in v1:
time: 351 us; the launch traced here: 350 us
  waiting for transfers between devices  202 us (58%)
  matrix products  69 us (20%)
  starting transfers between devices  25.6 us (7%)
  blocking collectives  20.2 us (6%)
  local copies, waits for them, and re-layouts  16.1 us (5%)
  between operations  14 us (4%)
    psum x1, waiting for transfers between devices, per_device(): grams = lax.psum(grams, ('pr', 'pc'))  114 us
    dot_general x31, matrix products, contract(): lax.dot_general(left_side, right_side, (((left_dim,), (right_dim,)), ((),...  69 us
    all_gather x2, waiting for transfers between devices, columns(): lax.all_gather(lax.ppermute(own, ('pr', 'pc'), moves), 'pr', axis=1, tile...  53.5 us
    ppermute x7, waiting for transfers between devices, per_device(): pieces = [lax.ppermute(pieces[0], 'pc', route), *pieces]  29.8 us
    all_gather x1, blocking collectives, per_device(): y_row = lax.all_gather(y_own, 'pc', axis=1, tiled=True)  20.2 us
    ppermute x7, starting transfers between devices, per_device(): pieces = [lax.ppermute(pieces[0], 'pc', route), *pieces]  13 us
    ppermute x2, starting transfers between devices, columns(): lax.ppermute(own, ('pr', 'pc'), moves)  12.5 us
  transfers between devices with their start and end apart: 13, of which 10 were waited for; matrix products, arithmetic and copies ran while one was open for 14% of the time, Pallas kernels for 0%

profile of v1, /device:TPU:1, one launch (start us, length us, event | category | flops | bytes accessed | tf_op | source)
XLA Modules:
  0.0 349.7 jit_solution(13596898895503419526)
XLA Ops:
  8.3 4.5 %collective-permute-start = (f32[192,160]{0,1:T(8,128)S(1)}, f32[192,160]{0,1:T(8,128)S(1)}, u32[]{:S(2)}, u32[]{:S(2)}) collective-permute-start(f32[192,160]{0,1:T(8,128)S(1)} %copy.12), channel_id=1, source_target_pairs={{0,0},{1,8},{2,16},{3,24},{4,32},{5,40},{6,48},{7,56},{8,64},{9,72... | collective-permute-start | bytes 368648 | tf_op jit(solution)/shard_map/ppermute | solution.py:55
  12.8 4.5 %collective-permute-done = f32[192,160]{0,1:T(8,128)S(1)} collective-permute-done((f32[192,160]{0,1:T(8,128)S(1)}, f32[192,160]{0,1:T(8,128)S(1)}, u32[]{:S(2)}, u32[]{:S(2)}) %collective-permute-start) | collective-permute-done | bytes 122912 | tf_op jit(solution)/shard_map/ppermute | solution.py:55
  18.0 53.5 %all-gather.3.cloned.1.call-done = f32[192,2560]{0,1:T(8,128)} async-done(((f32[192,160]{0,1:T(8,128)}), f32[192,2560]{0,1:T(8,128)}) %all-gather.3.cloned.1.call-update) | async-done | bytes 1966096 | tf_op jit(solution)/shard_map/all_gather | solution.py:55
  71.5 9.9 %fusion.110 = f32[192,1280]{0,1:T(8,128)} fusion(f32[192,2560]{0,1:T(8,128)} %all-gather.3.cloned.1.call-done, f32[1280,2560]{1,0:T(8,128)} %param.3), kind=kOutput, calls=%fused_computation.162 | convolution fusion | flops 3774873600 | bytes 16056320 | tf_op jit(solution)/shard_map/dot_general | solution.py:10
  81.5 2.1 collective-permute-start.1
  83.6 2.6 collective-permute-done.1
  86.2 2.5 collective-permute-start.2
  88.7 3.5 collective-permute-done.2
  92.2 2.5 collective-permute-start.3
  94.7 3.5 collective-permute-done.3
  98.2 2.7 collective-permute-start.4
  100.9 4.2 %collective-permute-done.4 = f32[192,160]{1,0:T(8,128)S(1)} collective-permute-done((f32[192,160]{1,0:T(8,128)S(1)}, f32[192,160]{1,0:T(8,128)S(1)}, u32[]{:S(2)}, u32[]{:S(2)}) %collective-permute-start.4) | collective-permute-done | bytes 122912 | tf_op jit(solution)/shard_map/ppermute | solution.py:61
  105.1 2.3 collective-permute-start.5
  107.3 4.9 %collective-permute-done.5 = f32[192,160]{1,0:T(8,128)S(1)} collective-permute-done((f32[192,160]{1,0:T(8,128)S(1)}, f32[192,160]{1,0:T(8,128)S(1)}, u32[]{:S(2)}, u32[]{:S(2)}) %collective-permute-start.5) | collective-permute-done | bytes 122912 | tf_op jit(solution)/shard_map/ppermute | solution.py:61
  113.2 5.4 %collective-permute-done.6 = f32[192,160]{1,0:T(8,128)S(1)} collective-permute-done((f32[192,160]{1,0:T(8,128)S(1)}, f32[192,160]{1,0:T(8,128)S(1)}, u32[]{:S(2)}, u32[]{:S(2)}) %collective-permute-start.6) | collective-permute-done | bytes 122912 | tf_op jit(solution)/shard_map/ppermute | solution.py:61
  119.2 5.7 %collective-permute-done.7 = f32[192,160]{1,0:T(8,128)} collective-permute-done((f32[192,160]{1,0:T(8,128)S(1)}, f32[192,160]{1,0:T(8,128)}, u32[]{:S(2)}, u32[]{:S(2)}) %collective-permute-start.7) | collective-permute-done | bytes 122912 | tf_op jit(solution)/shard_map/ppermute | solution.py:61
  125.0 2.5 concatenate.88
  127.6 2.7 convolution_bitcast_fusion
  130.3 8.0 %collective-permute-start.8 = (f32[192,160]{0,1:T(8,128)}, f32[192,160]{0,1:T(8,128)S(1)}, u32[]{:S(2)}, u32[]{:S(2)}) collective-permute-start(f32[192,160]{0,1:T(8,128)} %reduce-scatter.2.cloned.1.call-done), channel_id=1, source_target_pairs={{0,0},{1,8},{2,16},{3,24},{4,32},{5,40},{6,48},{7,56},{8,64},{9,72... | collective-permute-start | bytes 368648 | tf_op jit(solution)/shard_map/ppermute | solution.py:55
  138.3 20.2 %all_gather.10 = f32[192,1280]{0,1:T(8,128)} all-gather(f32[192,160]{0,1:T(8,128)} %reduce-scatter.2.cloned.1.call-done), channel_id=1, replica_groups=mesh['pr'=16,'pc'=8] {'pc'}, dimensions={1}, use_global_device_ids=true | all-gather | bytes 1105920 | tf_op jit(solution)/shard_map/all_gather | solution.py:68
  159.2 114.1 %all-reduce.2.cloned.1.call-done = f32[192,384]{1,0:T(8,128)} async-done(((f32[192,384]{1,0:T(8,128)}), f32[192,384]{1,0:T(8,128)}) %all-reduce.2.cloned.1.call-update) | async-done | bytes 294928 | tf_op jit(solution)/shard_map/psum | solution.py:71
  273.3 1.2 fusion.109
  274.6 1.2 pad_maximum_fusion.1
  284.7 1.2 convolution_subtract_fusion.3
  289.7 1.3 convolution_subtract_fusion.5
  294.1 1.5 convolution_subtract_fusion.4
  300.0 1.6 convolution_subtract_fusion.2
  305.3 1.7 convolution_subtract_fusion.1
  311.2 2.2 fusion.13
  313.5 2.9 fusion.35
  316.4 3.4 convolution_add_fusion
  319.8 23.4 %convolution_subtract_fusion = f32[1280,2560]{1,0:T(8,128)} fusion(f32[1280,2560]{1,0:T(8,128)} %param.3, f32[192,2560]{0,1:T(8,128)} %all-gather.5.cloned.1.call-done, f32[192,2560]{0,1:T(8,128)S(1)} %copy-done, f32[192,1280]{1,0:T(8,128)} %fusion.13, f32[192,1280]{1,0:T(8,128)} %convolution_add_fusion), kind=kOutput, calls=%fused_computation | convolution fusion | flops 7554498560 | bytes 32112640 | tf_op jit(solution)/shard_map/dot_general | solution.py:10
  (84 shorter events, 32.2 us)
Async XLA Ops:
  7.2 64.3 %all-gather.3.cloned.1.call-start = ((), (), s32[]{:S(2)}) async-start(), calls=%async_computation.1 | async-start | bytes 2785280 | tf_op jit(solution)/shard_map/all_gather | solution.py:55
  8.2 73.2 %copy-start.6 = (f32[192,160]{0,1:T(8,128)}, f32[192,160]{0,1:T(8,128)S(1)}, u32[]{:S(2)}) copy-start(f32[192,160]{0,1:T(8,128)S(1)} %copy.12) | copy-start | bytes 368644
  8.3 9.0 %collective-permute-start = (f32[192,160]{0,1:T(8,128)S(1)}, f32[192,160]{0,1:T(8,128)S(1)}, u32[]{:S(2)}, u32[]{:S(2)}) collective-permute-start(f32[192,160]{0,1:T(8,128)S(1)} %copy.12), channel_id=1, source_target_pairs={{0,0},{1,8},{2,16},{3,24},{4,32},{5,40},{6,48},{7,56},{8,64},{9,72... | collective-permute-start | bytes 368648 | tf_op jit(solution)/shard_map/ppermute | solution.py:55
  17.3 0.7 copy-start.8
  18.0 63.5 %copy-start.2 = (f32[6,32,160]{2,1,0:T(8,128)S(1)}, f32[6,32,160]{2,1,0:T(8,128)}, u32[]{:S(2)}) copy-start(f32[6,32,160]{2,1,0:T(8,128)} %param.4) | copy-start | bytes 368644
  18.0 109.6 %reduce-scatter.2.cloned.1.call-start = ((), (), s32[]{:S(2)}) async-start(), calls=%async_computation.2 | async-start | bytes 1474560 | tf_op jit(solution)/shard_map/reduce_scatter | solution.py:67
  81.5 191.9 %all-reduce.2.cloned.1.call-start = ((), (), s32[]{:S(2)}) async-start(), calls=%async_computation.3 | async-start | bytes 589824 | tf_op jit(solution)/shard_map/psum | solution.py:71
  81.5 4.7 %collective-permute-start.1 = (f32[192,160]{1,0:T(8,128)S(1)}, f32[192,160]{1,0:T(8,128)S(1)}, u32[]{:S(2)}, u32[]{:S(2)}) collective-permute-start(f32[192,160]{1,0:T(8,128)S(1)} %bitcast.69), channel_id=1, source_target_pairs={{0,1},{1,2},{2,3},{3,4},{4,5},{5,6},{6,7},{7,0},{8,9},{9,10},{10,1... | collective-permute-start | bytes 368648 | tf_op jit(solution)/shard_map/ppermute | solution.py:61
  86.2 6.0 %collective-permute-start.2 = (f32[192,160]{1,0:T(8,128)S(1)}, f32[192,160]{1,0:T(8,128)S(1)}, u32[]{:S(2)}, u32[]{:S(2)}) collective-permute-start(f32[192,160]{1,0:T(8,128)S(1)} %collective-permute-done.1), channel_id=1, source_target_pairs={{0,1},{1,2},{2,3},{3,4},{4,5},{5,6},{6,7},{7,0},{8,9},{9,10},{10,1... | collective-permute-start | bytes 368648 | tf_op jit(solution)/shard_map/ppermute | solution.py:61
  92.2 6.0 %collective-permute-start.3 = (f32[192,160]{1,0:T(8,128)S(1)}, f32[192,160]{1,0:T(8,128)S(1)}, u32[]{:S(2)}, u32[]{:S(2)}) collective-permute-start(f32[192,160]{1,0:T(8,128)S(1)} %collective-permute-done.2), channel_id=1, source_target_pairs={{0,1},{1,2},{2,3},{3,4},{4,5},{5,6},{6,7},{7,0},{8,9},{9,10},{10,1... | collective-permute-start | bytes 368648 | tf_op jit(solution)/shard_map/ppermute | solution.py:61
  98.2 6.9 %collective-permute-start.4 = (f32[192,160]{1,0:T(8,128)S(1)}, f32[192,160]{1,0:T(8,128)S(1)}, u32[]{:S(2)}, u32[]{:S(2)}) collective-permute-start(f32[192,160]{1,0:T(8,128)S(1)} %collective-permute-done.3), channel_id=1, source_target_pairs={{0,1},{1,2},{2,3},{3,4},{4,5},{5,6},{6,7},{7,0},{8,9},{9,10},{10,1... | collective-permute-start | bytes 368648 | tf_op jit(solution)/shard_map/ppermute | solution.py:61
  105.1 7.2 %collective-permute-start.5 = (f32[192,160]{1,0:T(8,128)S(1)}, f32[192,160]{1,0:T(8,128)S(1)}, u32[]{:S(2)}, u32[]{:S(2)}) collective-permute-start(f32[192,160]{1,0:T(8,128)S(1)} %collective-permute-done.4), channel_id=1, source_target_pairs={{0,1},{1,2},{2,3},{3,4},{4,5},{5,6},{6,7},{7,0},{8,9},{9,10},{10,1... | collective-permute-start | bytes 368648 | tf_op jit(solution)/shard_map/ppermute | solution.py:61
  112.2 6.3 %collective-permute-start.6 = (f32[192,160]{1,0:T(8,128)S(1)}, f32[192,160]{1,0:T(8,128)S(1)}, u32[]{:S(2)}, u32[]{:S(2)}) collective-permute-start(f32[192,160]{1,0:T(8,128)S(1)} %collective-permute-done.5), channel_id=1, source_target_pairs={{0,1},{1,2},{2,3},{3,4},{4,5},{5,6},{6,7},{7,0},{8,9},{9,10},{10,1... | collective-permute-start | bytes 368648 | tf_op jit(solution)/shard_map/ppermute | solution.py:61
  118.6 6.4 %collective-permute-start.7 = (f32[192,160]{1,0:T(8,128)S(1)}, f32[192,160]{1,0:T(8,128)}, u32[]{:S(2)}, u32[]{:S(2)}) collective-permute-start(f32[192,160]{1,0:T(8,128)S(1)} %collective-permute-done.6), channel_id=1, source_target_pairs={{0,1},{1,2},{2,3},{3,4},{4,5},{5,6},{6,7},{7,0},{8,9},{9,10},{10,1... | collective-permute-start | bytes 368648 | tf_op jit(solution)/shard_map/ppermute | solution.py:61
  127.5 183.7 %copy-start.1 = (f32[192,2560]{1,0:T(8,128)}, f32[192,2560]{1,0:T(8,128)S(1)}, u32[]{:S(2)}) copy-start(f32[192,2560]{1,0:T(8,128)S(1)} %concatenate.88) | copy-start | bytes 5898244
  130.3 189.5 %all-gather.5.cloned.1.call-start = ((), (), s32[]{:S(2)}) async-start(), calls=%async_computation.4 | async-start | bytes 2785280 | tf_op jit(solution)/shard_map/all_gather | solution.py:55
  130.3 28.2 %collective-permute-start.8 = (f32[192,160]{0,1:T(8,128)}, f32[192,160]{0,1:T(8,128)S(1)}, u32[]{:S(2)}, u32[]{:S(2)}) collective-permute-start(f32[192,160]{0,1:T(8,128)} %reduce-scatter.2.cloned.1.call-done), channel_id=1, source_target_pairs={{0,0},{1,8},{2,16},{3,24},{4,32},{5,40},{6,48},{7,56},{8,64},{9,72... | collective-permute-start | bytes 368648 | tf_op jit(solution)/shard_map/ppermute | solution.py:55
  158.5 0.7 copy-start.7
  273.3 6.1 %copy-start.5 = (f32[192,384]{1,0:T(8,128)S(1)}, f32[192,384]{1,0:T(8,128)}, u32[]{:S(2)}) copy-start(f32[192,384]{1,0:T(8,128)} %all-reduce.2.cloned.1.call-done) | copy-start | bytes 884740
  275.8 7.0 %copy-start.3 = (f32[192,576]{1,0:T(8,128)}, f32[192,576]{1,0:T(8,128)S(1)}, u32[]{:S(2)}) copy-start(f32[192,576]{1,0:T(8,128)S(1)} %get-tuple-element.5) | copy-start | bytes 1327108
  284.7 9.4 %copy-start.10 = (f32[96,32]{0,1:T(8,128)S(1)}, f32[96,32]{0,1:T(8,128)}, u32[]{:S(2)}) copy-start(f32[96,32]{0,1:T(8,128)} %copy.17) | copy-start | bytes 36868
  288.8 0.8 copy-start.9
  295.5 13.8 %copy-start.4 = (f32[192,160]{0,1:T(8,128)S(1)}, f32[192,160]{0,1:T(8,128)}, u32[]{:S(2)}) copy-start(f32[192,160]{0,1:T(8,128)} %reduce-scatter.2.cloned.1.call-done) | copy-start | bytes 368644
  313.5 6.3 %copy-start = (f32[192,2560]{0,1:T(8,128)S(1)}, f32[192,2560]{0,1:T(8,128)}, u32[]{:S(2)}) copy-start(f32[192,2560]{0,1:T(8,128)} %all-gather.3.cloned.1.call-done) | copy-start | bytes 5898244
Sparse Core Ops, SparseCore 0:
  18.1 53.3 all-gather.2
  81.6 30.1 reduce-scatter.1
  130.4 142.8 all-reduce.1
  275.3 44.3 all-gather.4
